TPU v7x, 512 devices: a whole 4x4x16 slice. The times are simulated.
512 devices in a mesh: section: 4 (over z_hi), dp: 8 (over x, core), tensor: 16 (over z_lo, y).
Axes of the slice: x: 4, y: 4, z: 16 (z_hi: 4, z_lo: 4; z = z_hi * 4 + z_lo), core: 2. Of those that a mesh axis runs over, the one named last changes fastest.
Arguments:
- hidden: bfloat16 [4, 1024, 28672], P('section', 'tensor', 'dp'), may hold values from -6 to 6
- down_weight: bfloat16 [4, 28672, 8192], P('section', 'dp', 'tensor'), may hold values from -0.03125 to 0.03125
- residual: bfloat16 [4, 1024, 8192], P('section', 'dp', 'tensor'), may hold values from -36 to 36
- norm_gain: float32 [4, 8192], P('section', 'tensor'), may hold values from 0.4 to 1.2
- query_weight: bfloat16 [4, 8192, 4096], P('section', 'tensor', 'dp'), may hold values from -0.0625 to 0.0625
- key_value_weight: bfloat16 [4, 8192, 2048], P('section', 'tensor', 'dp'), may hold values from -0.0625 to 0.0625
Outputs:
- attention: bfloat16 [4, 1024, 4096], P('section', 'tensor', 'dp')
All inputs are finite; a program needn't handle non-finite values.
Results may differ from a plain program's by a relative error of at most 0.04.
Values may be sent and summed in bfloat16 or wider, within the bound.
A program may use at most 64 MiB of HBM per device.

v0:
```python
import jax
import jax.numpy as jnp
from jax import lax
from jax.sharding import PartitionSpec as P

D = 8192
HD = 128
ROPE_BASE = 500000.0
EPSILON = 1e-05


def passed_along(value, axis, steps):
    count = lax.axis_size(axis)
    pairs = [(source, (source + steps) % count) for source in range(count)]
    return lax.ppermute(value, axis, pairs)


def rotate(values, positions):
    half_dim = values.shape[-1] // 2
    frequency = ROPE_BASE ** (-jnp.arange(half_dim, dtype=jnp.float32) * 2.0 / values.shape[-1])
    angles = positions.astype(jnp.float32)[:, None] * frequency[None, :]
    cosine = jnp.cos(angles)[:, None, :]
    sine_part = jnp.sin(angles)[:, None, :]
    front_part = values[..., :half_dim]
    back_part = values[..., half_dim:]
    return jnp.concatenate(
        [front_part * cosine - back_part * sine_part, back_part * cosine + front_part * sine_part],
        axis=-1,
    )


def per_device(hidden, down_weight, residual, norm_gain, query_weight, key_value_weight):
    weight_block = down_weight[0]
    partials = jnp.dot(
        lax.all_gather(hidden[0], "tensor", axis=0, tiled=True),
        weight_block,
        preferred_element_type=jnp.float32,
    )
    summed = lax.psum_scatter(
        partials.astype(jnp.bfloat16), "dp", scatter_dimension=0, tiled=True
    ).astype(jnp.float32)
    boundary = (residual[0].astype(jnp.float32) + summed).astype(jnp.bfloat16)
    gathered = lax.all_gather(boundary, "dp", axis=0, tiled=True)
    arrived = passed_along(gathered, "section", 1)
    values_in = arrived.astype(jnp.float32)
    squares = jnp.sum(values_in * values_in, axis=1)
    scaled = (values_in * norm_gain[0][None, :]).astype(jnp.bfloat16)
    query_sums = jnp.dot(scaled, query_weight[0], preferred_element_type=jnp.float32)
    pair_sums = jnp.dot(scaled, key_value_weight[0], preferred_element_type=jnp.float32)
    token_count = arrived.shape[0]
    own_rows = token_count // lax.axis_size("tensor")
    first_row = lax.axis_index("tensor") * own_rows
    query_sums, pair_sums, squares = (
        lax.psum(query_sums.astype(jnp.bfloat16), "tensor").astype(jnp.float32),
        lax.psum(pair_sums.astype(jnp.bfloat16), "tensor").astype(jnp.float32),
        lax.psum(squares.astype(jnp.bfloat16), "tensor").astype(jnp.float32),
    )
    query_local = lax.dynamic_slice_in_dim(query_sums, first_row, own_rows, 0)
    inverse = lax.rsqrt(squares / D + EPSILON)[:, None]
    positions = jnp.arange(token_count, dtype=jnp.int32)
    own_positions = first_row + jnp.arange(own_rows, dtype=jnp.int32)
    inverse_own = lax.dynamic_slice_in_dim(inverse, first_row, own_rows, 0)
    query_part = query_local * inverse_own
    queries = rotate(query_part.reshape(own_rows, -1, HD), own_positions).astype(jnp.bfloat16)
    pair_rows = (pair_sums * inverse).reshape(token_count, -1, 2, HD)
    key_rows = rotate(pair_rows[:, :, 0], positions).astype(jnp.bfloat16)
    value_rows = pair_rows[:, :, 1].astype(jnp.bfloat16)
    group_count = key_rows.shape[1]
    grouped = queries.reshape(own_rows, group_count, -1, HD)
    scores = jnp.einsum(
        "qgrd,kgd->grqk", grouped, key_rows, preferred_element_type=jnp.float32
    ) * HD ** (-0.5)
    causal = positions[None, :] <= own_positions[:, None]
    scores = jnp.where(causal[None, None], scores, -1e30)
    maximum = jnp.max(scores, axis=-1, keepdims=True)
    weights = jnp.exp(scores - maximum)
    probabilities = (weights / jnp.sum(weights, axis=-1, keepdims=True)).astype(jnp.bfloat16)
    attended = jnp.einsum(
        "grqk,kgd->qgrd", probabilities, value_rows, preferred_element_type=jnp.float32
    ).astype(jnp.bfloat16)
    return attended.reshape(own_rows, -1)[None]


def solution(mesh):
    placed = (
        P("section", "tensor", "dp"),
        P("section", "dp", "tensor"),
        P("section", "dp", "tensor"),
        P("section", "tensor"),
        P("section", "tensor", "dp"),
        P("section", "tensor", "dp"),
    )
    return jax.shard_map(
        per_device,
        mesh=mesh,
        in_specs=placed,
        out_specs=P("section", "tensor", "dp"),
        check_vma=False,
    )
```

profile of v0, /device:TPU:2, one launch (start us, length us, event | category | flops | bytes accessed | tf_op | source)
XLA Modules:
  0.0 486.2 jit_solution(7943351588400073942)
XLA Ops:
  6.5 0.7 all-gather.6.cloned.1.call-update
  7.3 0.0 reduce-scatter.2.cloned.1.call-start
  7.3 108.6 %all-gather.6.cloned.1.call-done = bf16[1,1024,3584]{2,1,0:T(8,128)(2,1)} async-done(((bf16[1,64,3584]{2,1,0:T(8,128)(2,1)}), bf16[1,1024,3584]{2,1,0:T(8,128)(2,1)}) %all-gather.6.cloned.1.call-update) | async-done | bytes 7340048 | tf_op jit(solution)/shard_map/all_gather | solution.py:35
  115.9 9.1 %fusion.5 = bf16[1024,512]{1,0:T(8,128)(2,1)} fusion(bf16[1,3584,512]{2,1,0:T(8,128)(2,1)} %param.7, bf16[1,1024,3584]{2,1,0:T(8,128)(2,1)} %all-gather.6.cloned.1.call-done), kind=kOutput, calls=%fused_computation.7 | convolution fusion | flops 3758620672 | bytes 12058624 | tf_op jit(solution)/shard_map/dot_general | solution.py:34
  125.0 0.0 reduce-scatter.2.cloned.1.call-update
  125.0 0.0 all-gather.4.cloned.1.call-start
  125.0 33.0 %reduce-scatter.2.cloned.1.call-done = bf16[128,512]{1,0:T(8,128)(2,1)} async-done(((bf16[1024,512]{1,0:T(8,128)(2,1)}), bf16[128,512]{1,0:T(8,128)(2,1)}) %reduce-scatter.2.cloned.1.call-update) | async-done | bytes 131088 | tf_op jit(solution)/shard_map/reduce_scatter | solution.py:39
  158.0 1.6 fusion.30
  159.6 0.0 all-reduce.3.cloned.1.call-start
  159.7 32.3 %all-gather.4.cloned.1.call-done = bf16[1024,512]{1,0:T(8,128)(2,1)} async-done(((bf16[128,512]{1,0:T(8,128)(2,1)}), bf16[1024,512]{1,0:T(8,128)(2,1)}) %all-gather.4.cloned.1.call-update) | async-done | bytes 1048592 | tf_op jit(solution)/shard_map/all_gather | solution.py:43
  192.0 7.2 %collective-permute-start = (bf16[1024,512]{1,0:T(8,128)(2,1)}, bf16[1024,512]{1,0:T(8,128)(2,1)S(1)}, u32[]{:S(2)}, u32[]{:S(2)}) collective-permute-start(bf16[1024,512]{1,0:T(8,128)(2,1)} %all-gather.4.cloned.1.call-done), channel_id=1, source_target_pairs={{0,128},{128,256},{256,384},{384,0},{1,129},{129,257},{257,385},{3... | collective-permute-start | bytes 3145736 | tf_op jit(solution)/shard_map/ppermute | solution.py:15
  199.2 55.4 %collective-permute-done = bf16[1024,512]{1,0:T(8,128)(2,1)S(1)} collective-permute-done((bf16[1024,512]{1,0:T(8,128)(2,1)}, bf16[1024,512]{1,0:T(8,128)(2,1)S(1)}, u32[]{:S(2)}, u32[]{:S(2)}) %collective-permute-start) | collective-permute-done | bytes 1048608 | tf_op jit(solution)/shard_map/ppermute | solution.py:15
  254.6 1.3 convolution_convert_fusion.1
  255.8 1.8 convolution_convert_fusion
  257.7 0.1 iota_compare_fusion
  257.8 0.2 multiply_cosine_fusion.1
  258.0 0.3 fusion.4
  258.2 79.6 %psum.22 = bf16[1024]{0:T(1024)(128)(2,1)S(1)} all-reduce(bf16[1024]{0:T(1024)(128)(2,1)S(1)} %fusion.4), channel_id=1, replica_groups=mesh['section'=4,'dp'=8,'tensor'=16] {'tensor'}, use_global_device_ids=true, to_apply=%region_3.0 | all-reduce | flops 1024 | bytes 4096 | tf_op jit(solution)/shard_map/psum | solution.py:56
  337.8 0.1 dynamic-slice.3
  337.9 133.5 %all-reduce.3.cloned.1.call-done = (bf16[1024,256]{1,0:T(8,128)(2,1)}, bf16[1024,512]{1,0:T(8,128)(2,1)}) async-done(((bf16[1024,256]{1,0:T(8,128)(2,1)}, bf16[1024,512]{1,0:T(8,128)(2,1)}), (bf16[1024,256]{1,0:T(8,128)(2,1)}, bf16[1024,512]{1,0:T(8,128)(2,1)})) %all-reduce.3.cloned.1.call-update) | async-done | bytes 1572880 | tf_op jit(solution)/shard_map/psum | solution.py:55
  471.5 1.2 convert_multiply_fusion.2
  472.7 0.5 reshape.223
  473.3 0.4 slice.26
  473.6 0.5 slice.25
  474.2 0.9 convert_multiply_fusion.3
  475.2 0.1 fusion.39
  475.3 2.4 fusion.33
  477.8 0.5 fusion.40
  478.3 0.3 fusion.13
  478.6 0.4 fusion.12
  479.0 0.1 copy.15
  479.1 0.7 broadcast_in_dim_reshape.3
  (18 shorter events, 0.2 us)
Async XLA Ops:
  6.5 249.3 %copy-start = (bf16[1,512,512]{2,1,0:T(8,128)(2,1)S(1)}, bf16[1,512,512]{2,1,0:T(8,128)(2,1)}, u32[]{:S(2)}) copy-start(bf16[1,512,512]{2,1,0:T(8,128)(2,1)} %param.10) | copy-start | bytes 1572868
  6.5 109.4 %all-gather.6.cloned.1.call-start = ((), (), s32[]{:S(2)}) async-start(), calls=%async_computation.3 | async-start | bytes 7798784 | tf_op jit(solution)/shard_map/all_gather | solution.py:35
  7.3 150.7 %copy-start.1 = (bf16[1,128,512]{2,1,0:T(8,128)(2,1)S(1)}, bf16[1,128,512]{2,1,0:T(8,128)(2,1)}, u32[]{:S(2)}) copy-start(bf16[1,128,512]{2,1,0:T(8,128)(2,1)} %param.8) | copy-start | bytes 393220
  7.3 247.3 %copy-start.2 = (bf16[1,512,256]{2,1,0:T(8,128)(2,1)S(1)}, bf16[1,512,256]{2,1,0:T(8,128)(2,1)}, u32[]{:S(2)}) copy-start(bf16[1,512,256]{2,1,0:T(8,128)(2,1)} %param.11) | copy-start | bytes 786436
  7.3 247.3 %copy-start.3 = (f32[1,512]{1,0:T(1,128)S(1)}, f32[1,512]{1,0:T(1,128)}, u32[]{:S(2)}) copy-start(f32[1,512]{1,0:T(1,128)} %param.9) | copy-start | bytes 6148
  7.3 150.7 %reduce-scatter.2.cloned.1.call-start = ((), (), s32[]{:S(2)}) async-start(), calls=%async_computation.1 | async-start | bytes 1179648 | tf_op jit(solution)/shard_map/reduce_scatter | solution.py:39
  125.0 67.0 %all-gather.4.cloned.1.call-start = ((), (), s32[]{:S(2)}) async-start(), calls=%async_computation.2 | async-start | bytes 1179648 | tf_op jit(solution)/shard_map/all_gather | solution.py:43
  159.6 311.9 %all-reduce.3.cloned.1.call-start = ((), (), s32[]{:S(2)}) async-start(), calls=%async_computation.4 | async-start | bytes 3145728 | tf_op jit(solution)/shard_map/psum | solution.py:55
  192.0 62.6 %collective-permute-start = (bf16[1024,512]{1,0:T(8,128)(2,1)}, bf16[1024,512]{1,0:T(8,128)(2,1)S(1)}, u32[]{:S(2)}, u32[]{:S(2)}) collective-permute-start(bf16[1024,512]{1,0:T(8,128)(2,1)} %all-gather.4.cloned.1.call-done), channel_id=1, source_target_pairs={{0,128},{128,256},{256,384},{384,0},{1,129},{129,257},{257,385},{3... | collective-permute-start | bytes 3145736 | tf_op jit(solution)/shard_map/ppermute | solution.py:15
Sparse Core Ops, SparseCore 0:
  9.4 106.4 all-gather.5
  125.1 32.8 reduce-scatter.1
  160.1 31.7 all-gather.3
  257.7 213.6 all-reduce.2
where the time goes:
time: 486 us
  waiting for transfers between devices  364 us (75%)
  blocking collectives  79.6 us (16%)
  between operations  13.3 us (3%)
  matrix products  12.9 us (3%)
  starting transfers between devices  7.32 us (2%)
  other arithmetic  7.13 us (1%)
    psum x1, waiting for transfers between devices, per_device(): lax.psum(pair_sums.astype(jnp.bfloat16), 'tensor').astype(jnp.float32)  134 us
    all_gather x1, waiting for transfers between devices, per_device(): lax.all_gather(hidden[0], 'tensor', axis=0, tiled=True)  109 us
    psum x1, blocking collectives, per_device(): lax.psum(squares.astype(jnp.bfloat16), 'tensor').astype(jnp.float32)  79.6 us
    ppermute x1, waiting for transfers between devices, passed_along(): return lax.ppermute(value, axis, pairs)  55.4 us
    reduce_scatter x1, waiting for transfers between devices, per_device(): lax.psum_scatter(partials.astype(jnp.bfloat16), 'dp', scatter_dimension=0...  33 us
    all_gather x1, waiting for transfers between devices, per_device(): gathered = lax.all_gather(boundary, 'dp', axis=0, tiled=True)  32.3 us
  transfers between devices with their start and end apart: 5, of which 5 were waited for; matrix products, arithmetic and copies ran while one was open for 0% of the time, Pallas kernels for 0%

commit v1 on v0

--- a/solution.py
+++ b/solution.py
@@ -7,6 +7,17 @@
 HD = 128
 ROPE_BASE = 500000.0
 EPSILON = 1e-05
+
+
+def pass_along(x, name, along):
+    size = lax.axis_size(name)
+    right = [(i, (i + 1) % size) for i in range(size)]
+    parts = [x]
+    for reach in range(1, size):
+        parts = [lax.ppermute(parts[0], name, right), *parts]
+    result = jnp.concatenate(parts, axis=along)
+    shift = (lax.axis_index(name) + 1) * parts[-1].shape[along]
+    return jnp.roll(result, shift, axis=along)
 
 
 def passed_along(value, axis, steps):
@@ -40,7 +51,7 @@
         partials.astype(jnp.bfloat16), "dp", scatter_dimension=0, tiled=True
     ).astype(jnp.float32)
     boundary = (residual[0].astype(jnp.float32) + summed).astype(jnp.bfloat16)
-    gathered = lax.all_gather(boundary, "dp", axis=0, tiled=True)
+    gathered = pass_along(boundary, "dp", 0)
     arrived = passed_along(gathered, "section", 1)
     values_in = arrived.astype(jnp.float32)
     squares = jnp.sum(values_in * values_in, axis=1)

time: 486 us -> 489 us (level)
    ppermute x0 -> x7, waiting for transfers between devices: none -> 35.2 us  [pass_along(): parts = [lax.ppermute(parts[0], name, right), *parts]]
    all_gather x1 -> x0, waiting for transfers between devices: 32.3 us -> none  [per_device(): gathered = lax.all_gather(boundary, 'dp', axis=0, tiled=True)]
  transfers between devices with their start and end apart: 5 -> 11, of which waited for: 5 -> 11; matrix products, arithmetic and copies ran while one was open for 0% -> 0% of each run, Pallas kernels for 0% -> 0%
where the time goes in v1:
time: 489 us
  waiting for transfers between devices  366 us (75%)
  blocking collectives  79.6 us (16%)
  between operations  13.4 us (3%)
  matrix products  12.9 us (3%)
  starting transfers between devices  7.94 us (2%)
  other arithmetic  6.48 us (1%)
    psum x1, waiting for transfers between devices, per_device(): lax.psum(pair_sums.astype(jnp.bfloat16), 'tensor').astype(jnp.float32)  138 us
    all_gather x1, waiting for transfers between devices, per_device(): lax.all_gather(hidden[0], 'tensor', axis=0, tiled=True)  109 us
    psum x1, blocking collectives, per_device(): lax.psum(squares.astype(jnp.bfloat16), 'tensor').astype(jnp.float32)  79.6 us
    ppermute x1, waiting for transfers between devices, passed_along(): return lax.ppermute(value, axis, pairs)  50.6 us
    ppermute x7, waiting for transfers between devices, pass_along(): parts = [lax.ppermute(parts[0], name, right), *parts]  35.2 us
    reduce_scatter x1, waiting for transfers between devices, per_device(): lax.psum_scatter(partials.astype(jnp.bfloat16), 'dp', scatter_dimension=0...  33 us
  transfers between devices with their start and end apart: 11, of which 11 were waited for; matrix products, arithmetic and copies ran while one was open for 0% of the time, Pallas kernels for 0%

profile of v1, /device:TPU:2, one launch (start us, length us, event | category | flops | bytes accessed | tf_op | source)
XLA Modules:
  0.0 489.1 jit_solution(20431677967576334)
XLA Ops:
  6.5 0.7 all-gather.3.cloned.1.call-update
  7.3 108.6 %all-gather.3.cloned.1.call-done = bf16[1,1024,3584]{2,1,0:T(8,128)(2,1)} async-done(((bf16[1,64,3584]{2,1,0:T(8,128)(2,1)}), bf16[1,1024,3584]{2,1,0:T(8,128)(2,1)}) %all-gather.3.cloned.1.call-update) | async-done | bytes 7340048 | tf_op jit(solution)/shard_map/all_gather | solution.py:46
  115.9 9.1 %fusion.5 = bf16[1024,512]{1,0:T(8,128)(2,1)} fusion(bf16[1,3584,512]{2,1,0:T(8,128)(2,1)} %param.7, bf16[1,1024,3584]{2,1,0:T(8,128)(2,1)} %all-gather.3.cloned.1.call-done), kind=kOutput, calls=%fused_computation.7 | convolution fusion | flops 3758620672 | bytes 12058624 | tf_op jit(solution)/shard_map/dot_general | solution.py:45
  125.1 33.0 %reduce-scatter.2.cloned.1.call-done = bf16[128,512]{1,0:T(8,128)(2,1)} async-done(((bf16[1024,512]{1,0:T(8,128)(2,1)}), bf16[128,512]{1,0:T(8,128)(2,1)}) %reduce-scatter.2.cloned.1.call-update) | async-done | bytes 131088 | tf_op jit(solution)/shard_map/reduce_scatter | solution.py:50
  158.0 0.9 fusion.30
  159.0 4.4 collective-permute-done
  163.4 4.4 collective-permute-done.1
  167.7 4.4 collective-permute-done.2
  172.1 5.3 %collective-permute-done.3 = bf16[128,512]{1,0:T(8,128)(2,1)S(1)} collective-permute-done((bf16[128,512]{1,0:T(8,128)(2,1)S(1)}, bf16[128,512]{1,0:T(8,128)(2,1)S(1)}, u32[]{:S(2)}, u32[]{:S(2)}) %collective-permute-start.3) | collective-permute-done | bytes 131104 | tf_op jit(solution)/shard_map/ppermute | solution.py:17
  177.4 5.6 %collective-permute-done.4 = bf16[128,512]{1,0:T(8,128)(2,1)S(1)} collective-permute-done((bf16[128,512]{1,0:T(8,128)(2,1)S(1)}, bf16[128,512]{1,0:T(8,128)(2,1)S(1)}, u32[]{:S(2)}, u32[]{:S(2)}) %collective-permute-start.4) | collective-permute-done | bytes 131104 | tf_op jit(solution)/shard_map/ppermute | solution.py:17
  183.0 5.6 %collective-permute-done.5 = bf16[128,512]{1,0:T(8,128)(2,1)S(1)} collective-permute-done((bf16[128,512]{1,0:T(8,128)(2,1)S(1)}, bf16[128,512]{1,0:T(8,128)(2,1)S(1)}, u32[]{:S(2)}, u32[]{:S(2)}) %collective-permute-start.5) | collective-permute-done | bytes 131104 | tf_op jit(solution)/shard_map/ppermute | solution.py:17
  188.6 5.6 %collective-permute-done.6 = bf16[128,512]{1,0:T(8,128)(2,1)S(1)} collective-permute-done((bf16[128,512]{1,0:T(8,128)(2,1)S(1)}, bf16[128,512]{1,0:T(8,128)(2,1)S(1)}, u32[]{:S(2)}, u32[]{:S(2)}) %collective-permute-start.6) | collective-permute-done | bytes 131104 | tf_op jit(solution)/shard_map/ppermute | solution.py:17
  194.6 7.8 %collective-permute-start.7 = (bf16[1024,512]{1,0:T(8,128)(2,1)S(1)}, bf16[1024,512]{1,0:T(8,128)(2,1)S(1)}, u32[]{:S(2)}, u32[]{:S(2)}) collective-permute-start(bf16[1024,512]{1,0:T(8,128)(2,1)S(1)} %constant_dynamic-slice_fusion), channel_id=1, source_target_pairs={{0,128},{128,256},{256,384},{384,0},{1,129},{129,257},{257,385},{3... | collective-permute-start | bytes 3145736 | tf_op jit(solution)/shard_map/ppermute | solution.py:26
  202.5 50.6 %collective-permute-done.7 = bf16[1024,512]{1,0:T(8,128)(2,1)S(1)} collective-permute-done((bf16[1024,512]{1,0:T(8,128)(2,1)S(1)}, bf16[1024,512]{1,0:T(8,128)(2,1)S(1)}, u32[]{:S(2)}, u32[]{:S(2)}) %collective-permute-start.7) | collective-permute-done | bytes 1048608 | tf_op jit(solution)/shard_map/ppermute | solution.py:26
  253.1 1.7 convolution_convert_fusion
  254.8 1.3 convolution_convert_fusion.1
  256.1 0.1 iota_compare_fusion
  256.3 0.2 multiply_cosine_fusion.1
  256.5 0.3 fusion.4
  256.7 79.6 %psum.22 = bf16[1024]{0:T(1024)(128)(2,1)S(1)} all-reduce(bf16[1024]{0:T(1024)(128)(2,1)S(1)} %fusion.4), channel_id=1, replica_groups=mesh['section'=4,'dp'=8,'tensor'=16] {'tensor'}, use_global_device_ids=true, to_apply=%region_3.4 | all-reduce | flops 1024 | bytes 4096 | tf_op jit(solution)/shard_map/psum | solution.py:67
  336.4 138.0 %all-reduce.3.cloned.1.call-done = (bf16[1024,256]{1,0:T(8,128)(2,1)}, bf16[1024,512]{1,0:T(8,128)(2,1)}) async-done(((bf16[1024,256]{1,0:T(8,128)(2,1)}, bf16[1024,512]{1,0:T(8,128)(2,1)}), (bf16[1024,256]{1,0:T(8,128)(2,1)}, bf16[1024,512]{1,0:T(8,128)(2,1)})) %all-reduce.3.cloned.1.call-update) | async-done | bytes 1572880 | tf_op jit(solution)/shard_map/psum | solution.py:66
  474.4 1.2 convert_multiply_fusion.2
  475.6 0.5 reshape.223
  476.2 0.4 slice.26
  476.5 0.5 slice.25
  477.1 0.9 convert_multiply_fusion.3
  478.1 0.1 fusion.39
  478.2 2.4 fusion.33
  480.7 0.5 fusion.40
  481.2 0.3 fusion.13
  481.5 0.4 fusion.12
  482.0 0.7 broadcast_in_dim_reshape.3
  (46 shorter events, 0.7 us)
Async XLA Ops:
  6.5 246.6 %copy-start = (bf16[1,512,512]{2,1,0:T(8,128)(2,1)S(1)}, bf16[1,512,512]{2,1,0:T(8,128)(2,1)}, u32[]{:S(2)}) copy-start(bf16[1,512,512]{2,1,0:T(8,128)(2,1)} %param.10) | copy-start | bytes 1572868
  6.5 109.4 %all-gather.3.cloned.1.call-start = ((), (), s32[]{:S(2)}) async-start(), calls=%async_computation.2 | async-start | bytes 7798784 | tf_op jit(solution)/shard_map/all_gather | solution.py:46
  7.3 150.7 %copy-start.1 = (bf16[1,128,512]{2,1,0:T(8,128)(2,1)S(1)}, bf16[1,128,512]{2,1,0:T(8,128)(2,1)}, u32[]{:S(2)}) copy-start(bf16[1,128,512]{2,1,0:T(8,128)(2,1)} %param.8) | copy-start | bytes 393220
  7.3 150.7 %reduce-scatter.2.cloned.1.call-start = ((), (), s32[]{:S(2)}) async-start(), calls=%async_computation.1 | async-start | bytes 1179648 | tf_op jit(solution)/shard_map/reduce_scatter | solution.py:50
  125.0 349.4 %all-reduce.3.cloned.1.call-start = ((), (), s32[]{:S(2)}) async-start(), calls=%async_computation.3 | async-start | bytes 3145728 | tf_op jit(solution)/shard_map/psum | solution.py:66
  158.9 4.4 collective-permute-start
  163.4 4.4 collective-permute-start.1
  167.7 4.4 collective-permute-start.2
  172.1 5.3 %collective-permute-start.3 = (bf16[128,512]{1,0:T(8,128)(2,1)S(1)}, bf16[128,512]{1,0:T(8,128)(2,1)S(1)}, u32[]{:S(2)}, u32[]{:S(2)}) collective-permute-start(bf16[128,512]{1,0:T(8,128)(2,1)S(1)} %collective-permute-done.2), channel_id=1, source_target_pairs={{0,16},{16,32},{32,48},{48,64},{64,80},{80,96},{96,112},{112,0},{1... | collective-permute-start | bytes 393224 | tf_op jit(solution)/shard_map/ppermute | solution.py:17
  177.4 5.6 %collective-permute-start.4 = (bf16[128,512]{1,0:T(8,128)(2,1)S(1)}, bf16[128,512]{1,0:T(8,128)(2,1)S(1)}, u32[]{:S(2)}, u32[]{:S(2)}) collective-permute-start(bf16[128,512]{1,0:T(8,128)(2,1)S(1)} %collective-permute-done.3), channel_id=1, source_target_pairs={{0,16},{16,32},{32,48},{48,64},{64,80},{80,96},{96,112},{112,0},{1... | collective-permute-start | bytes 393224 | tf_op jit(solution)/shard_map/ppermute | solution.py:17
  183.0 5.6 %collective-permute-start.5 = (bf16[128,512]{1,0:T(8,128)(2,1)S(1)}, bf16[128,512]{1,0:T(8,128)(2,1)S(1)}, u32[]{:S(2)}, u32[]{:S(2)}) collective-permute-start(bf16[128,512]{1,0:T(8,128)(2,1)S(1)} %collective-permute-done.4), channel_id=1, source_target_pairs={{0,16},{16,32},{32,48},{48,64},{64,80},{80,96},{96,112},{112,0},{1... | collective-permute-start | bytes 393224 | tf_op jit(solution)/shard_map/ppermute | solution.py:17
  188.6 5.6 %collective-permute-start.6 = (bf16[128,512]{1,0:T(8,128)(2,1)S(1)}, bf16[128,512]{1,0:T(8,128)(2,1)S(1)}, u32[]{:S(2)}, u32[]{:S(2)}) collective-permute-start(bf16[128,512]{1,0:T(8,128)(2,1)S(1)} %collective-permute-done.5), channel_id=1, source_target_pairs={{0,16},{16,32},{32,48},{48,64},{64,80},{80,96},{96,112},{112,0},{1... | collective-permute-start | bytes 393224 | tf_op jit(solution)/shard_map/ppermute | solution.py:17
  194.4 58.7 %copy-start.3 = (f32[1,512]{1,0:T(1,128)S(1)}, f32[1,512]{1,0:T(1,128)}, u32[]{:S(2)}) copy-start(f32[1,512]{1,0:T(1,128)} %param.9) | copy-start | bytes 6148
  194.6 60.2 %copy-start.2 = (bf16[1,512,256]{2,1,0:T(8,128)(2,1)S(1)}, bf16[1,512,256]{2,1,0:T(8,128)(2,1)}, u32[]{:S(2)}) copy-start(bf16[1,512,256]{2,1,0:T(8,128)(2,1)} %param.11) | copy-start | bytes 786436
  194.6 58.5 %collective-permute-start.7 = (bf16[1024,512]{1,0:T(8,128)(2,1)S(1)}, bf16[1024,512]{1,0:T(8,128)(2,1)S(1)}, u32[]{:S(2)}, u32[]{:S(2)}) collective-permute-start(bf16[1024,512]{1,0:T(8,128)(2,1)S(1)} %constant_dynamic-slice_fusion), channel_id=1, source_target_pairs={{0,128},{128,256},{256,384},{384,0},{1,129},{129,257},{257,385},{3... | collective-permute-start | bytes 3145736 | tf_op jit(solution)/shard_map/ppermute | solution.py:26
Sparse Core Ops, SparseCore 0:
  9.4 106.4 all-gather.2
  125.1 32.8 reduce-scatter.1
  256.2 218.1 all-reduce.2
